TPU v7x, 32 devices: a whole 2x2x4 slice. The times are simulated.
32 devices in a mesh: member: 8 (over z, x), tensor: 4 (over y, core).
Axes of the slice: x: 2, y: 2, z: 4, core: 2. Of those that a mesh axis runs over, the one named last changes fastest.
Arguments:
- tokens: bfloat16 [1024, 8192], P('member'), may hold values from -6 to 6
- out_grad: bfloat16 [1024, 8192], P('member'), may hold values from -6 to 6
- flip_bits: int32 [1024], P('member'), may hold values 0 or 1
- in_scale: float32 [8, 8192], P(None, 'member'), may hold values from 0.5 to 2
- out_scale: float32 [8, 8192], P(None, 'member'), may hold values from 0.5 to 2
- gate_scale: float32 [8, 14336], P('member', 'tensor'), may hold values from 0.5 to 2
- gate_flip: float32 [8, 14336], P('member', 'tensor'), may hold values from -2 to 2
- up_scale: float32 [8, 14336], P('member', 'tensor'), may hold values from 0.5 to 2
- up_flip: float32 [8, 14336], P('member', 'tensor'), may hold values from -2 to 2
- proj_gate: bfloat16 [1024, 14336], P('member', 'tensor'), may hold values from -6 to 6
- proj_up: bfloat16 [1024, 14336], P('member', 'tensor'), may hold values from -6 to 6
- w_gate: bfloat16 [8192, 14336], P('member', 'tensor'), may hold values from -0.0625 to 0.0625
- w_up: bfloat16 [8192, 14336], P('member', 'tensor'), may hold values from -0.0625 to 0.0625
- w_down: bfloat16 [14336, 8192], P('tensor', 'member'), may hold values from -0.046875 to 0.046875
Outputs:
- x_grad: bfloat16 [1024, 8192], P(('member', 'tensor'))
- w_gate_grad: bfloat16 [8192, 14336], P('member', 'tensor')
- w_up_grad: bfloat16 [8192, 14336], P('member', 'tensor')
- w_down_grad: bfloat16 [14336, 8192], P('tensor', 'member')
- in_scale_grad: float32 [8, 8192], P(None, 'member')
- out_scale_grad: float32 [8, 8192], P(None, 'member')
- gate_scale_grad: float32 [8, 14336], P('member', 'tensor')
- gate_flip_grad: float32 [8, 14336], P('member', 'tensor')
- up_scale_grad: float32 [8, 14336], P('member', 'tensor')
- up_flip_grad: float32 [8, 14336], P('member', 'tensor')
All inputs are finite; a program needn't handle non-finite values. No bound on the sum of `flip_bits` on one device may be relied on, other than what follows from the above.
Results may differ from a plain program's by a relative error of at most 0.024.
Values may be sent and summed in bfloat16 or wider, within the bound.
A program may use at most 128 MiB of HBM per device.

v0:
```python
import jax
import jax.numpy as jnp
from jax import lax
from jax.sharding import PartitionSpec as P


def scale_rows(block, table, rows):
    members, width = table.shape
    scaled = block.reshape(members, rows, width).astype(jnp.float32) * table[:, None, :]
    return scaled.reshape(members * rows, width)


def contract_rows(left, right):
    return lax.dot_general(
        left, right, (((0,), (0,)), ((), ())), preferred_element_type=jnp.float32
    )


def contract_cols(left, right):
    return lax.dot_general(
        left, right, (((1,), (1,)), ((), ())), preferred_element_type=jnp.float32
    )


def local(
    tokens,
    out_grad,
    flip_bits,
    in_scale,
    out_scale,
    gate_scale,
    gate_flip,
    up_scale,
    up_flip,
    proj_gate,
    proj_up,
    w_gate,
    w_up,
    w_down,
):
    rows = tokens.shape[0]
    members, width = in_scale.shape
    tensor_count = lax.axis_size("tensor")
    all_tokens, all_cotan = (
        lax.all_to_all(tokens, "member", split_axis=1, concat_axis=0, tiled=True),
        lax.all_to_all(out_grad, "member", split_axis=1, concat_axis=0, tiled=True),
    )
    in_rows = scale_rows(all_tokens, in_scale, rows).astype(jnp.bfloat16)
    grad_z = scale_rows(all_cotan, out_scale, rows).astype(jnp.bfloat16)
    grad_hidden = lax.psum_scatter(
        contract_cols(grad_z, w_down).astype(jnp.bfloat16),
        "member",
        scatter_dimension=0,
        tiled=True,
    ).astype(jnp.float32)
    sign = (2 * flip_bits - 1).astype(jnp.float32)[:, None]
    gate_factor = gate_scale + sign * gate_flip
    up_factor = up_scale + sign * up_flip
    pg_f = proj_gate.astype(jnp.float32)
    pu_f = proj_up.astype(jnp.float32)
    gate = pg_f * gate_factor
    up = pu_f * up_factor
    sig = jax.nn.sigmoid(gate)
    act = gate * sig
    hidden = (act * up).astype(jnp.bfloat16)
    grad_gate = grad_hidden * up * sig * (1.0 + gate * (1.0 - sig))
    grad_up = grad_hidden * act
    gate_scale_grad = jnp.sum(grad_gate * pg_f, axis=0, keepdims=True)
    gate_flip_grad = jnp.sum(sign * grad_gate * pg_f, axis=0, keepdims=True)
    up_scale_grad = jnp.sum(grad_up * pu_f, axis=0, keepdims=True)
    up_flip_grad = jnp.sum(sign * grad_up * pu_f, axis=0, keepdims=True)
    grad_pg = (grad_gate * gate_factor).astype(jnp.bfloat16)
    grad_pu = (grad_up * up_factor).astype(jnp.bfloat16)
    hid_piece = lax.all_gather(hidden, "member", axis=0, tiled=True)
    pg_piece = lax.all_gather(grad_pg, "member", axis=0, tiled=True)
    pu_piece = lax.all_gather(grad_pu, "member", axis=0, tiled=True)
    count = hid_piece.shape[0]
    groups = count // rows
    down_acc = contract_rows(hid_piece, grad_z)
    gate_acc = contract_rows(in_rows, pg_piece)
    up_acc = contract_rows(in_rows, pu_piece)
    grad_piece = contract_cols(pg_piece, w_gate) + contract_cols(pu_piece, w_up)
    grad_in = grad_piece
    in_terms = (
        (all_tokens.astype(jnp.float32) * grad_piece).reshape(groups, rows, width).sum(axis=1)
    )
    in_part = in_terms
    down_piece = jnp.dot(hid_piece, w_down, preferred_element_type=jnp.float32)
    out_terms = (
        (all_cotan.astype(jnp.float32) * down_piece).reshape(groups, rows, width).sum(axis=1)
    )
    out_part = out_terms
    down_acc, gate_acc, up_acc, grad_in, in_part, out_part = (
        down_acc,
        gate_acc,
        up_acc,
        grad_in,
        in_part,
        out_part,
    )
    in_scale_grad, out_scale_grad = (
        lax.psum(in_part.astype(jnp.bfloat16), "tensor").astype(jnp.float32),
        lax.psum(out_part.astype(jnp.bfloat16), "tensor").astype(jnp.float32),
    )
    scaled = grad_in.reshape(members, rows, width) * in_scale[:, None, :]
    summed = lax.psum_scatter(
        scaled.astype(jnp.bfloat16), "tensor", scatter_dimension=1, tiled=True
    ).astype(jnp.float32)
    returned = lax.all_to_all(
        summed.astype(jnp.bfloat16), "member", split_axis=0, concat_axis=2, tiled=True
    ).astype(summed.dtype)
    x_grad = returned.reshape(rows // tensor_count, members * width).astype(jnp.bfloat16)
    return (
        x_grad,
        gate_acc.astype(jnp.bfloat16),
        up_acc.astype(jnp.bfloat16),
        down_acc.astype(jnp.bfloat16),
        in_scale_grad,
        out_scale_grad,
        gate_scale_grad,
        gate_flip_grad,
        up_scale_grad,
        up_flip_grad,
    )


def solution(mesh):
    return jax.shard_map(
        local,
        mesh=mesh,
        in_specs=(
            P("member", None),
            P("member", None),
            P("member"),
            P(None, "member"),
            P(None, "member"),
            P("member", "tensor"),
            P("member", "tensor"),
            P("member", "tensor"),
            P("member", "tensor"),
            P("member", "tensor"),
            P("member", "tensor"),
            P("member", "tensor"),
            P("member", "tensor"),
            P("tensor", "member"),
        ),
        out_specs=(
            P(("member", "tensor"), None),
            P("member", "tensor"),
            P("member", "tensor"),
            P("tensor", "member"),
            P(None, "member"),
            P(None, "member"),
            P("member", "tensor"),
            P("member", "tensor"),
            P("member", "tensor"),
            P("member", "tensor"),
        ),
        check_vma=False,
    )
```

profile of v0, /device:TPU:0, one launch (start us, length us, event | category | flops | bytes accessed | tf_op | source)
XLA Modules:
  0.0 658.5 jit_solution(12860040867740411838)
XLA Ops:
  7.2 0.0 reduce-scatter.3.cloned.1.call-start
  7.2 1.8 copy.34
  9.0 0.0 copy-start.5
  9.0 0.0 copy-start.10
  9.0 55.6 %all_to_all.44 = bf16[128,8,1024]{2,0,1:T(8,128)(2,1)S(1)} all-to-all(bf16[128,8,1024]{2,0,1:T(8,128)(2,1)S(1)} %bitcast.57), channel_id=1, replica_groups=mesh['member'=8,'tensor'=4] {'member'}, dimensions={1} | all-to-all | bytes 4194304 | tf_op jit(solution)/shard_map/all_to_all | solution.py:46
  64.6 0.0 copy-done.5
  64.6 0.5 fusion
  65.1 0.0 copy-start.1
  65.2 1.4 copy-done.1
  66.5 0.0 copy-done.10
  66.5 9.9 %convolution_convert_fusion.3 = bf16[1024,3584]{1,0:T(8,128)(2,1)} fusion(bf16[1024,1024]{1,0:T(8,128)(2,1)S(1)} %fusion, bf16[3584,1024]{1,0:T(8,128)(2,1)S(1)} %copy-done.10), kind=kOutput, calls=%fused_computation.3 | convolution fusion | flops 7519862784 | bytes 16777216 | tf_op jit(solution)/shard_map/dot_general | solution.py:20
  76.4 0.0 copy-start.6
  76.4 0.0 copy-start.7
  76.4 0.0 copy-start.8
  76.4 0.0 copy-start.9
  76.4 0.0 copy-start.12
  76.4 0.0 copy-start.3
  76.4 0.0 reduce-scatter.3.cloned.1.call-update
  76.4 0.0 all-gather.4.cloned.1.call-start
  76.5 0.6 copy-done.6
  77.1 0.0 copy-done.7
  77.2 0.0 copy-done.8
  77.2 0.0 copy-done.9
  77.3 0.0 copy-done.12
  77.3 131.2 %reduce-scatter.3.cloned.1.call-done = bf16[128,3584]{1,0:T(8,128)(2,1)} async-done(((bf16[1024,3584]{1,0:T(8,128)(2,1)}), bf16[128,3584]{1,0:T(8,128)(2,1)}) %reduce-scatter.3.cloned.1.call-update) | async-done | bytes 917520 | tf_op jit(solution)/shard_map/reduce_scatter | solution.py:50
  208.5 0.0 copy-done.3
  208.5 4.4 fusion.5
  212.9 1.2 multiply_convert_fusion.3
  214.1 0.0 all-gather.4.cloned.1.call-update
  214.2 0.0 all-gather.6.cloned.1.call-start
  214.2 0.7 all-gather.6.cloned.1.call-update
  214.9 0.0 all-gather.8.cloned.1.call-start
  214.9 0.5 all-gather.8.cloned.1.call-update
  215.5 0.0 reduce-scatter.5.cloned.1.call-start
  215.5 1.8 copy.33
  217.3 0.0 copy-start.4
  217.3 81.4 %all_to_all.45 = bf16[128,8,1024]{2,0,1:T(8,128)(2,1)S(1)} all-to-all(bf16[128,8,1024]{2,0,1:T(8,128)(2,1)S(1)} %bitcast.58), channel_id=1, replica_groups=mesh['member'=8,'tensor'=4] {'member'}, dimensions={1} | all-to-all | bytes 4194304 | tf_op jit(solution)/shard_map/all_to_all | solution.py:45
  298.8 0.0 copy-done.4
  298.8 0.0 copy-start
  298.8 2.1 fusion.1
  300.9 0.0 copy-done
  300.9 0.6 broadcast_in_dim.16
  301.5 0.6 broadcast_in_dim.17
  302.1 0.6 broadcast_in_dim.18
  302.7 0.6 broadcast_in_dim.19
  303.3 57.7 %all-gather.4.cloned.1.call-done = bf16[1024,3584]{1,0:T(8,128)(2,1)} async-done(((bf16[128,3584]{1,0:T(8,128)(2,1)}), bf16[1024,3584]{1,0:T(8,128)(2,1)}) %all-gather.4.cloned.1.call-update) | async-done | bytes 7340048 | tf_op jit(solution)/shard_map/all_gather | solution.py:75
  361.0 13.5 %fusion.10 = f32[1024,1024]{1,0:T(8,128)} fusion(bf16[1024,3584]{1,0:T(8,128)(2,1)} %all-gather.4.cloned.1.call-done, bf16[1024,3584]{1,0:T(8,128)(2,1)} %param.25), kind=kOutput, calls=%fused_computation.38 | convolution fusion | flops 7516192768 | bytes 18874368 | tf_op jit(solution)/shard_map/dot_general | solution.py:20
  374.4 98.8 %all-gather.6.cloned.1.call-done = bf16[1024,3584]{1,0:T(8,128)(2,1)} async-done(((bf16[128,3584]{1,0:T(8,128)(2,1)}), bf16[1024,3584]{1,0:T(8,128)(2,1)}) %all-gather.6.cloned.1.call-update) | async-done | bytes 7340048 | tf_op jit(solution)/shard_map/all_gather | solution.py:76
  473.2 13.5 %bitcast_reduce_fusion.1 = (bf16[8,1024]{1,0:T(8,128)(2,1)S(1)}, f32[1024,1024]{1,0:T(8,128)S(1)}) fusion(bf16[128,8,1024]{2,0,1:T(8,128)(2,1)} %copy-done, f32[1024,1024]{1,0:T(8,128)} %fusion.10, bf16[1024,3584]{1,0:T(8,128)(2,1)} %all-gather.6.cloned.1.call-done, bf16[1024,3584]{1,0:T(8,128)(2,1)} %param.26), kind=kOutput, calls=%fused_computation.8 | convolution fusion | flops 7520378880 | bytes 25182208 | tf_op jit(solution)/shard_map/dot_general | solution.py:20
  486.7 1.9 multiply_convert_fusion
  488.7 0.0 reduce-scatter.5.cloned.1.call-update
  488.7 96.8 %all-gather.8.cloned.1.call-done = bf16[1024,3584]{1,0:T(8,128)(2,1)} async-done(((bf16[128,3584]{1,0:T(8,128)(2,1)}), bf16[1024,3584]{1,0:T(8,128)(2,1)}) %all-gather.8.cloned.1.call-update) | async-done | bytes 7340048 | tf_op jit(solution)/shard_map/all_gather | solution.py:74
  585.5 12.2 %bitcast_reduce_fusion = bf16[8,1024]{1,0:T(8,128)(2,1)S(1)} fusion(bf16[128,8,1024]{2,0,1:T(8,128)(2,1)S(1)} %all_to_all.44, bf16[1024,3584]{1,0:T(8,128)(2,1)} %all-gather.8.cloned.1.call-done, bf16[3584,1024]{1,0:T(8,128)(2,1)} %param.27), kind=kOutput, calls=%fused_computation.4 | convolution fusion | flops 7519330304 | bytes 16793600 | tf_op jit(solution)/shard_map/dot_general | solution.py:88
  597.7 11.4 %all-reduce = (bf16[8,1024]{1,0:T(8,128)(2,1)S(1)}, bf16[8,1024]{1,0:T(8,128)(2,1)S(1)}) all-reduce(bf16[8,1024]{1,0:T(8,128)(2,1)S(1)} %get-tuple-element.21, bf16[8,1024]{1,0:T(8,128)(2,1)S(1)} %bitcast_reduce_fusion), channel_id=1, replica_groups=mesh['member'=8,'tensor'=4] {'tensor'}, use_global_device_ids=true, to_apply=%region_3.0 | all-reduce | flops 16384 | bytes 65536 | tf_op jit(solution)/shard_map/psum | solution.py:102
  609.1 0.6 convert_element_type.104
  609.8 0.6 convert_element_type.106
  610.4 12.8 %convolution_convert_fusion.2 = bf16[1024,3584]{1,0:T(8,128)(2,1)} fusion(bf16[1024,1024]{1,0:T(8,128)(2,1)} %fusion.1, bf16[1024,3584]{1,0:T(8,128)(2,1)} %all-gather.4.cloned.1.call-done), kind=kOutput, calls=%fused_computation.2 | convolution fusion | flops 7519862784 | bytes 16777216 | tf_op jit(solution)/shard_map/dot_general | solution.py:14
  623.2 0.0 copy-done.2
  623.2 0.0 copy-done.11
  623.2 10.0 %convolution_convert_fusion = bf16[3584,1024]{1,0:T(8,128)(2,1)} fusion(bf16[1024,3584]{1,0:T(8,128)(2,1)S(1)} %copy-done.11, bf16[1024,1024]{1,0:T(8,128)(2,1)S(1)} %copy-done.2), kind=kOutput, calls=%fused_computation | convolution fusion | flops 7519862784 | bytes 16777216 | tf_op jit(solution)/shard_map/dot_general | solution.py:14
  633.2 3.8 all-to-all-start.1
  637.0 12.7 %convolution_convert_fusion.1 = bf16[1024,3584]{1,0:T(8,128)(2,1)} fusion(bf16[1024,1024]{1,0:T(8,128)(2,1)} %fusion.1, bf16[1024,3584]{1,0:T(8,128)(2,1)} %all-gather.6.cloned.1.call-done), kind=kOutput, calls=%fused_computation.1 | convolution fusion | flops 7519862784 | bytes 16777216 | tf_op jit(solution)/shard_map/dot_general | solution.py:14
  649.6 1.5 all-to-all-done.1
  651.2 0.8 copy.29
  (8 shorter events, 0.2 us)
Async XLA Ops:
  7.2 201.3 %reduce-scatter.3.cloned.1.call-start = ((), (), s32[]{:S(2)}) async-start(), calls=%async_computation.5 | async-start | bytes 8257536 | tf_op jit(solution)/shard_map/reduce_scatter | solution.py:50
  9.0 55.6 %copy-start.5 = (f32[8,1024]{1,0:T(8,128)S(1)}, f32[8,1024]{1,0:T(8,128)}, u32[]{:S(2)}) copy-start(f32[8,1024]{1,0:T(8,128)} %param.18) | copy-start | bytes 98308
  9.0 57.5 %copy-start.10 = (bf16[3584,1024]{1,0:T(8,128)(2,1)S(1)}, bf16[3584,1024]{1,0:T(8,128)(2,1)}, u32[]{:S(2)}) copy-start(bf16[3584,1024]{1,0:T(8,128)(2,1)} %param.27) | copy-start | bytes 22020100
  65.1 1.4 copy-start.1
  76.4 0.7 copy-start.6
  76.4 0.8 copy-start.7
  76.4 0.8 copy-start.8
  76.4 0.9 copy-start.9
  76.4 0.9 copy-start.12
  76.4 132.1 %copy-start.3 = (bf16[128,3584]{1,0:T(8,128)(2,1)S(1)}, bf16[128,3584]{1,0:T(8,128)(2,1)}, u32[]{:S(2)}) copy-start(bf16[128,3584]{1,0:T(8,128)(2,1)} %param.24) | copy-start | bytes 2752516
  76.4 284.5 %all-gather.4.cloned.1.call-start = ((), (), s32[]{:S(2)}) async-start(), calls=%async_computation.6 | async-start | bytes 8257536 | tf_op jit(solution)/shard_map/all_gather | solution.py:75
  214.2 259.1 %all-gather.6.cloned.1.call-start = ((), (), s32[]{:S(2)}) async-start(), calls=%async_computation.7 | async-start | bytes 8257536 | tf_op jit(solution)/shard_map/all_gather | solution.py:76
  214.9 370.6 %all-gather.8.cloned.1.call-start = ((), (), s32[]{:S(2)}) async-start(), calls=%async_computation.9 | async-start | bytes 8257536 | tf_op jit(solution)/shard_map/all_gather | solution.py:74
  215.5 417.7 %reduce-scatter.5.cloned.1.call-start = ((), (), s32[]{:S(2)}) async-start(), calls=%async_computation.8 | async-start | bytes 2621440 | tf_op jit(solution)/shard_map/reduce_scatter | solution.py:106
  217.3 81.4 %copy-start.4 = (f32[8,1024]{1,0:T(8,128)S(1)}, f32[8,1024]{1,0:T(8,128)}, u32[]{:S(2)}) copy-start(f32[8,1024]{1,0:T(8,128)} %param.17) | copy-start | bytes 98308
  298.8 2.1 copy-start
  610.4 12.8 %copy-start.2 = (bf16[1024,1024]{1,0:T(8,128)(2,1)S(1)}, bf16[1024,1024]{1,0:T(8,128)(2,1)}, u32[]{:S(2)}) copy-start(bf16[1024,1024]{1,0:T(8,128)(2,1)} %copy-done.1) | copy-start | bytes 6291460
  610.4 12.8 %copy-start.11 = (bf16[1024,3584]{1,0:T(8,128)(2,1)S(1)}, bf16[1024,3584]{1,0:T(8,128)(2,1)}, u32[]{:S(2)}) copy-start(bf16[1024,3584]{1,0:T(8,128)(2,1)} %all-gather.8.cloned.1.call-done) | copy-start | bytes 22020100
  633.2 18.0 %all-to-all-start.1 = ((bf16[8,32,1024]{2,1,0:T(8,128)(2,1)}), bf16[8,32,1024]{2,1,0:T(8,128)(2,1)S(1)}, u32[]{:S(2)}, u32[]{:S(2)}) async-start(bf16[8,32,1024]{2,1,0:T(8,128)(2,1)} %reduce-scatter.5.cloned.1.call-done), calls=%async_computation.3 | async-start | bytes 1048576 | tf_op jit(solution)/shard_map/all_to_all | solution.py:109
Sparse Core Ops, SparseCore 0:
  76.5 131.8 reduce-scatter.2
  214.3 146.6 all-gather.3
  363.2 110.0 all-gather.5
  475.8 109.6 all-gather.7
  588.5 29.6 reduce-scatter.4
where the time goes:
time: 659 us
  waiting for transfers between devices  387 us (59%)
  blocking collectives  148 us (22%)
  matrix products  84.5 us (13%)
  between operations  14 us (2%)
  other arithmetic  11.6 us (2%)
  local copies, waits for them, and re-layouts  8.85 us (1%)
    reduce_scatter x1, waiting for transfers between devices, local(): lax.psum_scatter(contract_cols(grad_z, w_down).astype(jnp.bfloat16), 'mem...  131 us
    all_gather x1, waiting for transfers between devices, local(): pu_piece = lax.all_gather(grad_pu, 'member', axis=0, tiled=True)  98.8 us
    all_gather x1, waiting for transfers between devices, local(): hid_piece = lax.all_gather(hidden, 'member', axis=0, tiled=True)  96.8 us
    all_to_all x1, blocking collectives, local(): lax.all_to_all(tokens, 'member', split_axis=1, concat_axis=0, tiled=True)  81.4 us
    all_gather x1, waiting for transfers between devices, local(): pg_piece = lax.all_gather(grad_pg, 'member', axis=0, tiled=True)  57.7 us
    all_to_all x1, blocking collectives, local(): lax.all_to_all(out_grad, 'member', split_axis=1, concat_axis=0, tiled=True)  55.6 us
    dot_general x3, matrix products, contract_cols(): lax.dot_general(left, right, (((1,), (1,)), ((), ())), preferred_element_...  36.8 us
    dot_general x3, matrix products, contract_rows(): lax.dot_general(left, right, (((0,), (0,)), ((), ())), preferred_element_...  35.5 us
  transfers between devices with their start and end apart: 6, of which 5 were waited for; matrix products, arithmetic and copies ran while one was open for 13% of the time, Pallas kernels for 0%

commit v1 on v0

--- a/solution.py
+++ b/solution.py
@@ -2,6 +2,13 @@
 import jax.numpy as jnp
 from jax import lax
 from jax.sharding import PartitionSpec as P
+
+
+def group_ways_for(values, row_dim):
+    values = jnp.moveaxis(values, 0, row_dim)
+    tmp = values.shape
+    front = values.reshape(*tmp[:row_dim], tmp[row_dim] * tmp[row_dim + 1], *tmp[row_dim + 2 :])
+    return front
 
 
 def scale_rows(block, table, rows):
@@ -73,7 +80,14 @@
     grad_pu = (grad_up * up_factor).astype(jnp.bfloat16)
     hid_piece = lax.all_gather(hidden, "member", axis=0, tiled=True)
     pg_piece = lax.all_gather(grad_pg, "member", axis=0, tiled=True)
-    pu_piece = lax.all_gather(grad_pu, "member", axis=0, tiled=True)
+    devs = jax.lax.psum(1, "member")
+    series = [(dev, (dev + 1) % devs) for dev in range(devs)]
+    views = [grad_pu]
+    while len(views) < devs:
+        views.append(jax.lax.ppermute(views[-1], "member", series))
+    e_next = jax.lax.axis_index("member")
+    views = jnp.stack(views, 0)[(e_next - jnp.arange(devs)) % devs]
+    pu_piece = group_ways_for(views, 0)
     count = hid_piece.shape[0]
     groups = count // rows
     down_acc = contract_rows(hid_piece, grad_z)

time: 659 us -> 673 us (1.021)
  blocking collectives: 148 us -> 67 us
  starting transfers between devices: 3.95 us -> 67.2 us
  local copies, waits for them, and re-layouts: 8.85 us -> 30.6 us
  other arithmetic: 11.6 us -> 19.2 us
    ppermute x0 -> x7, waiting for transfers between devices: none -> 119 us  [local(): views.append(jax.lax.ppermute(views[-1], 'member', series))]
    all_gather x1 -> x0, waiting for transfers between devices: 98.8 us -> none  [local(): pu_piece = lax.all_gather(grad_pu, 'member', axis=0, tiled=True)]
    all_to_all x1 -> x0, blocking collectives: 81.4 us -> none  [local(): lax.all_to_all(tokens, 'member', split_axis=1, concat_axis=0, tiled=True)]
    all_to_all x0 -> x1, waiting for transfers between devices: none -> 71.7 us  [local(): lax.all_to_all(tokens, 'member', split_axis=1, concat_axis=0, tiled=True)]
    ppermute x0 -> x7, starting transfers between devices: none -> 59.8 us  [local(): views.append(jax.lax.ppermute(views[-1], 'member', series))]
    all_gather x1, waiting for transfers between devices: 57.7 us -> 0.01 us  [local(): pg_piece = lax.all_gather(grad_pg, 'member', axis=0, tiled=True)]
    all_gather x1, waiting for transfers between devices: 96.8 us -> 64.2 us  [local(): hid_piece = lax.all_gather(hidden, 'member', axis=0, tiled=True)]
    gather x0 -> x1, local copies, waits for them, and re-layouts: none -> 7.15 us  [local(): views = jnp.stack(views, 0)[(e_next - jnp.arange(devs)) % devs]]
  transfers between devices with their start and end apart: 6 -> 13, of which waited for: 5 -> 10; matrix products, arithmetic and copies ran while one was open for 13% -> 17% of each run, Pallas kernels for 0% -> 0%
where the time goes in v1:
time: 673 us; the launch traced here: 672 us
  waiting for transfers between devices  388 us (58%)
  matrix products  86 us (13%)
  starting transfers between devices  67.2 us (10%)
  blocking collectives  67 us (10%)
  local copies, waits for them, and re-layouts  30.6 us (5%)
  other arithmetic  19.2 us (3%)
  between operations  14 us (2%)
    reduce_scatter x1, waiting for transfers between devices, local(): lax.psum_scatter(contract_cols(grad_z, w_down).astype(jnp.bfloat16), 'mem...  131 us
    ppermute x7, waiting for transfers between devices, local(): views.append(jax.lax.ppermute(views[-1], 'member', series))  119 us
    all_to_all x1, waiting for transfers between devices, local(): lax.all_to_all(tokens, 'member', split_axis=1, concat_axis=0, tiled=True)  71.7 us
    all_gather x1, waiting for transfers between devices, local(): hid_piece = lax.all_gather(hidden, 'member', axis=0, tiled=True)  64.2 us
    ppermute x7, starting transfers between devices, local(): views.append(jax.lax.ppermute(views[-1], 'member', series))  59.8 us
    all_to_all x1, blocking collectives, local(): lax.all_to_all(out_grad, 'member', split_axis=1, concat_axis=0, tiled=True)  55.6 us
    dot_general x3, matrix products, contract_rows(): lax.dot_general(left, right, (((0,), (0,)), ((), ())), preferred_element_...  38.8 us
    dot_general x3, matrix products, contract_cols(): lax.dot_general(left, right, (((1,), (1,)), ((), ())), preferred_element_...  34.8 us
  transfers between devices with their start and end apart: 13, of which 10 were waited for; matrix products, arithmetic and copies ran while one was open for 17% of the time, Pallas kernels for 0%

profile of v1, /device:TPU:0, one launch (start us, length us, event | category | flops | bytes accessed | tf_op | source)
XLA Modules:
  0.0 672.3 jit_solution(3255910337599807434)
XLA Ops:
  7.2 0.0 reduce-scatter.3.cloned.1.call-start
  7.2 1.8 copy.33
  9.0 0.0 copy-start.12
  9.0 55.6 %all_to_all.44 = bf16[128,8,1024]{2,0,1:T(8,128)(2,1)S(1)} all-to-all(bf16[128,8,1024]{2,0,1:T(8,128)(2,1)S(1)} %bitcast.78), channel_id=1, replica_groups=mesh['member'=8,'tensor'=4] {'member'}, dimensions={1} | all-to-all | bytes 4194304 | tf_op jit(solution)/shard_map/all_to_all | solution.py:53
  64.6 0.5 fusion.1
  65.2 1.4 copy-done.5
  66.6 9.9 %convolution_convert_fusion.2 = bf16[1024,3584]{1,0:T(8,128)(2,1)} fusion(bf16[1024,1024]{1,0:T(8,128)(2,1)S(1)} %fusion.1, bf16[3584,1024]{1,0:T(8,128)(2,1)S(1)} %copy-done.12), kind=kOutput, calls=%fused_computation.4 | convolution fusion | flops 7519862784 | bytes 16777216 | tf_op jit(solution)/shard_map/dot_general | solution.py:27
  76.5 0.0 copy-start.11
  76.5 0.0 copy-start.13
  76.5 0.0 reduce-scatter.3.cloned.1.call-update
  76.5 0.0 all-gather.3.cloned.1.call-start
  76.6 0.6 copy-done.8
  77.4 131.2 %reduce-scatter.3.cloned.1.call-done = bf16[128,3584]{1,0:T(8,128)(2,1)} async-done(((bf16[1024,3584]{1,0:T(8,128)(2,1)}), bf16[128,3584]{1,0:T(8,128)(2,1)}) %reduce-scatter.3.cloned.1.call-update) | async-done | bytes 917520 | tf_op jit(solution)/shard_map/reduce_scatter | solution.py:57
  208.6 4.2 fusion.9
  212.8 1.2 multiply_convert_fusion.3
  214.0 0.0 all-gather.3.cloned.1.call-update
  214.0 4.1 copy.28
  218.1 3.7 all-to-all-start.2
  221.8 0.0 all-gather.5.cloned.1.call-start
  221.8 0.7 all-gather.5.cloned.1.call-update
  222.5 0.0 reduce-scatter.5.cloned.1.call-start
  222.6 3.5 bitcast_dynamic-update-slice_fusion.7
  226.0 1.9 collective-permute-start
  228.0 71.7 %all-to-all-done.2 = bf16[128,8,1024]{0,2,1:T(8,128)(2,1)S(1)} async-done(((bf16[128,8,1024]{0,2,1:T(8,128)(2,1)}), bf16[128,8,1024]{0,2,1:T(8,128)(2,1)S(1)}, u32[]{:S(2)}, u32[]{:S(2)}) %all-to-all-start.2) | async-done | bytes 2097184 | tf_op jit(solution)/shard_map/all_to_all | solution.py:52
  299.7 2.3 convert_bitcast_fusion
  302.0 5.4 copy.27
  307.4 4.1 fusion.2
  311.5 0.6 broadcast_in_dim.8
  312.1 0.6 broadcast_in_dim.18
  312.7 0.6 broadcast_in_dim.19
  313.3 0.6 broadcast_in_dim.20
  314.0 39.6 %collective-permute-start.1 = (bf16[128,3584]{1,0:T(8,128)(2,1)S(1)}, bf16[128,3584]{1,0:T(8,128)(2,1)S(1)}, u32[]{:S(2)}, u32[]{:S(2)}) collective-permute-start(bf16[128,3584]{1,0:T(8,128)(2,1)S(1)} %collective-permute-done), channel_id=1, source_target_pairs={{0,4},{4,8},{8,12},{12,16},{16,20},{20,24},{24,28},{28,0},{1,5},{5... | collective-permute-start | bytes 2752520 | tf_op jit(solution)/shard_map/ppermute | solution.py:87
  353.5 1.0 bitcast_dynamic-update-slice_fusion.6
  354.5 21.1 %collective-permute-done.1 = bf16[128,3584]{1,0:T(8,128)(2,1)S(1)} collective-permute-done((bf16[128,3584]{1,0:T(8,128)(2,1)S(1)}, bf16[128,3584]{1,0:T(8,128)(2,1)S(1)}, u32[]{:S(2)}, u32[]{:S(2)}) %collective-permute-start.1) | collective-permute-done | bytes 917536 | tf_op jit(solution)/shard_map/ppermute | solution.py:87
  375.6 16.1 %collective-permute-start.2 = (bf16[128,3584]{1,0:T(8,128)(2,1)S(1)}, bf16[128,3584]{1,0:T(8,128)(2,1)S(1)}, u32[]{:S(2)}, u32[]{:S(2)}) collective-permute-start(bf16[128,3584]{1,0:T(8,128)(2,1)S(1)} %collective-permute-done.1), channel_id=1, source_target_pairs={{0,4},{4,8},{8,12},{12,16},{16,20},{20,24},{24,28},{28,0},{1,5},{5... | collective-permute-start | bytes 2752520 | tf_op jit(solution)/shard_map/ppermute | solution.py:87
  391.7 1.0 bitcast_dynamic-update-slice_fusion.5
  392.7 24.6 %collective-permute-done.2 = bf16[128,3584]{1,0:T(8,128)(2,1)S(1)} collective-permute-done((bf16[128,3584]{1,0:T(8,128)(2,1)S(1)}, bf16[128,3584]{1,0:T(8,128)(2,1)S(1)}, u32[]{:S(2)}, u32[]{:S(2)}) %collective-permute-start.2) | collective-permute-done | bytes 917536 | tf_op jit(solution)/shard_map/ppermute | solution.py:87
  417.2 1.5 collective-permute-start.3
  418.7 1.0 bitcast_dynamic-update-slice_fusion.4
  419.7 18.0 %collective-permute-done.3 = bf16[128,3584]{1,0:T(8,128)(2,1)S(1)} collective-permute-done((bf16[128,3584]{1,0:T(8,128)(2,1)S(1)}, bf16[128,3584]{1,0:T(8,128)(2,1)S(1)}, u32[]{:S(2)}, u32[]{:S(2)}) %collective-permute-start.3) | collective-permute-done | bytes 917536 | tf_op jit(solution)/shard_map/ppermute | solution.py:87
  437.7 1.0 bitcast_dynamic-update-slice_fusion.3
  438.7 19.5 %collective-permute-done.4 = bf16[128,3584]{1,0:T(8,128)(2,1)S(1)} collective-permute-done((bf16[128,3584]{1,0:T(8,128)(2,1)S(1)}, bf16[128,3584]{1,0:T(8,128)(2,1)S(1)}, u32[]{:S(2)}, u32[]{:S(2)}) %collective-permute-start.4) | collective-permute-done | bytes 917536 | tf_op jit(solution)/shard_map/ppermute | solution.py:87
  458.3 1.0 bitcast_dynamic-update-slice_fusion.2
  459.2 19.5 %collective-permute-done.5 = bf16[128,3584]{1,0:T(8,128)(2,1)S(1)} collective-permute-done((bf16[128,3584]{1,0:T(8,128)(2,1)S(1)}, bf16[128,3584]{1,0:T(8,128)(2,1)S(1)}, u32[]{:S(2)}, u32[]{:S(2)}) %collective-permute-start.5) | collective-permute-done | bytes 917536 | tf_op jit(solution)/shard_map/ppermute | solution.py:87
  478.8 0.7 collective-permute-start.6
  479.5 1.0 bitcast_dynamic-update-slice_fusion.1
  480.5 16.3 %collective-permute-done.6 = bf16[128,3584]{1,0:T(8,128)(2,1)S(1)} collective-permute-done((bf16[128,3584]{1,0:T(8,128)(2,1)S(1)}, bf16[128,3584]{1,0:T(8,128)(2,1)S(1)}, u32[]{:S(2)}, u32[]{:S(2)}) %collective-permute-start.6) | collective-permute-done | bytes 917536 | tf_op jit(solution)/shard_map/ppermute | solution.py:87
  496.7 1.0 bitcast_dynamic-update-slice_fusion
  497.7 7.1 %gather_fusion = bf16[8,128,3584]{2,1,0:T(8,128)(2,1)} fusion(bf16[8,128,3584]{2,1,0:T(8,128)(2,1)} %bitcast_dynamic-update-slice_fusion, s32[1024]{0:T(1024)S(1)} %pad_clamp_fusion), kind=kCustom, calls=%fused_computation | custom fusion | bytes 14680096 | tf_op jit(solution)/shard_map/gather | solution.py:89
  504.9 14.2 %fusion.16 = f32[1024,1024]{1,0:T(8,128)} fusion(bf16[1024,3584]{1,0:T(8,128)(2,1)} %all-gather.3.cloned.1.call-done, bf16[1024,3584]{1,0:T(8,128)(2,1)} %param.25), kind=kOutput, calls=%fused_computation.58 | convolution fusion | flops 7516192768 | bytes 18874368 | tf_op jit(solution)/shard_map/dot_general | solution.py:27
  519.1 10.8 %bitcast_reduce_fusion.1 = (bf16[8,1024]{1,0:T(8,128)(2,1)S(1)}, f32[1024,1024]{1,0:T(8,128)S(1)}) fusion(f32[8,128,1024]{2,1,0:T(8,128)S(1)} %copy-done, f32[1024,1024]{1,0:T(8,128)} %fusion.16, bf16[1024,3584]{1,0:T(8,128)(2,1)S(1)} %bitcast.79, bf16[1024,3584]{1,0:T(8,128)(2,1)} %param.26), kind=kOutput, calls=%fused_computation.12 | convolution fusion | flops 7519330304 | bytes 27279360 | tf_op jit(solution)/shard_map/dot_general | solution.py:27
  529.8 2.0 multiply_convert_fusion
  531.8 0.0 reduce-scatter.5.cloned.1.call-update
  531.8 13.0 %bitcast_convert_fusion = bf16[1024,3584]{1,0:T(8,128)(2,1)} fusion(bf16[8,128,3584]{2,1,0:T(8,128)(2,1)} %gather_fusion, bf16[128,8,1024]{0,2,1:T(8,128)(2,1)S(1)} %all-to-all-done.2, f32[8,1024]{1,0:T(8,128)S(1)} %copy-done.6), kind=kOutput, calls=%fused_computation.1 | convolution fusion | flops 7523008512 | bytes 16809984 | tf_op jit(solution)/shard_map/dot_general | solution.py:21
  544.8 64.2 %all-gather.5.cloned.1.call-done = bf16[1024,3584]{1,0:T(8,128)(2,1)} async-done(((bf16[128,3584]{1,0:T(8,128)(2,1)}), bf16[1024,3584]{1,0:T(8,128)(2,1)}) %all-gather.5.cloned.1.call-update) | async-done | bytes 7340048 | tf_op jit(solution)/shard_map/all_gather | solution.py:81
  609.0 12.4 %bitcast_reduce_fusion = bf16[8,1024]{1,0:T(8,128)(2,1)S(1)} fusion(bf16[128,8,1024]{2,0,1:T(8,128)(2,1)} %copy-done.1, bf16[1024,3584]{1,0:T(8,128)(2,1)} %all-gather.5.cloned.1.call-done, bf16[3584,1024]{1,0:T(8,128)(2,1)} %param.27), kind=kOutput, calls=%fused_computation.8 | convolution fusion | flops 7519330304 | bytes 16793600 | tf_op jit(solution)/shard_map/dot_general | solution.py:102
  621.4 11.4 %all-reduce = (bf16[8,1024]{1,0:T(8,128)(2,1)S(1)}, bf16[8,1024]{1,0:T(8,128)(2,1)S(1)}) all-reduce(bf16[8,1024]{1,0:T(8,128)(2,1)S(1)} %get-tuple-element.22, bf16[8,1024]{1,0:T(8,128)(2,1)S(1)} %bitcast_reduce_fusion), channel_id=1, replica_groups=mesh['member'=8,'tensor'=4] {'tensor'}, use_global_device_ids=true, to_apply=%region_3.0 | all-reduce | flops 16384 | bytes 65536 | tf_op jit(solution)/shard_map/psum | solution.py:116
  632.9 0.6 convert_element_type.117
  633.5 0.6 convert_element_type.119
  634.1 12.8 %convolution_convert_fusion = bf16[3584,1024]{1,0:T(8,128)(2,1)} fusion(bf16[1024,3584]{1,0:T(8,128)(2,1)} %all-gather.5.cloned.1.call-done, bf16[1024,1024]{1,0:T(8,128)(2,1)} %copy-done.5), kind=kOutput, calls=%fused_computation.2 | convolution fusion | flops 7519862784 | bytes 16777216 | tf_op jit(solution)/shard_map/dot_general | solution.py:21
  646.9 3.5 all-to-all-start.1
  650.4 13.0 %convolution_convert_fusion.1 = bf16[1024,3584]{1,0:T(8,128)(2,1)} fusion(bf16[1024,1024]{1,0:T(8,128)(2,1)S(1)} %copy-done.4, bf16[1024,3584]{1,0:T(8,128)(2,1)} %all-gather.3.cloned.1.call-done), kind=kOutput, calls=%fused_computation.3 | convolution fusion | flops 7519862784 | bytes 16777216 | tf_op jit(solution)/shard_map/dot_general | solution.py:21
  663.4 1.6 all-to-all-done.1
  664.9 0.8 copy.30
  (35 shorter events, 0.2 us)
Async XLA Ops:
  7.2 201.4 %reduce-scatter.3.cloned.1.call-start = ((), (), s32[]{:S(2)}) async-start(), calls=%async_computation.5 | async-start | bytes 8257536 | tf_op jit(solution)/shard_map/reduce_scatter | solution.py:57
  7.2 57.4 %copy-start.7 = (f32[8,1024]{1,0:T(8,128)S(1)}, f32[8,1024]{1,0:T(8,128)}, u32[]{:S(2)}) copy-start(f32[8,1024]{1,0:T(8,128)} %param.18) | copy-start | bytes 98308
  9.0 57.6 %copy-start.12 = (bf16[3584,1024]{1,0:T(8,128)(2,1)S(1)}, bf16[3584,1024]{1,0:T(8,128)(2,1)}, u32[]{:S(2)}) copy-start(bf16[3584,1024]{1,0:T(8,128)(2,1)} %param.27) | copy-start | bytes 22020100
  64.6 11.8 %copy-start.1 = (bf16[128,8,1024]{2,0,1:T(8,128)(2,1)}, bf16[128,8,1024]{2,0,1:T(8,128)(2,1)S(1)}, u32[]{:S(2)}) copy-start(bf16[128,8,1024]{2,0,1:T(8,128)(2,1)S(1)} %all_to_all.44) | copy-start | bytes 6291460
  65.2 1.4 copy-start.5
  76.4 0.7 copy-start.8
  76.4 0.8 copy-start.9
  76.4 0.8 copy-start.10
  76.5 0.9 copy-start.11
  76.5 0.9 copy-start.13
  76.5 132.1 %copy-start.3 = (bf16[128,3584]{1,0:T(8,128)(2,1)S(1)}, bf16[128,3584]{1,0:T(8,128)(2,1)}, u32[]{:S(2)}) copy-start(bf16[128,3584]{1,0:T(8,128)(2,1)} %param.23) | copy-start | bytes 2752516
  76.5 428.3 %all-gather.3.cloned.1.call-start = ((), (), s32[]{:S(2)}) async-start(), calls=%async_computation.6 | async-start | bytes 8257536 | tf_op jit(solution)/shard_map/all_gather | solution.py:82
  218.1 81.6 %all-to-all-start.2 = ((bf16[128,8,1024]{0,2,1:T(8,128)(2,1)}), bf16[128,8,1024]{0,2,1:T(8,128)(2,1)S(1)}, u32[]{:S(2)}, u32[]{:S(2)}) async-start(bf16[128,8,1024]{0,2,1:T(8,128)(2,1)} %bitcast.77), calls=%async_computation.4 | async-start | bytes 4194304 | tf_op jit(solution)/shard_map/all_to_all | solution.py:52
  221.8 387.2 %all-gather.5.cloned.1.call-start = ((), (), s32[]{:S(2)}) async-start(), calls=%async_computation.8 | async-start | bytes 8257536 | tf_op jit(solution)/shard_map/all_gather | solution.py:81
  222.5 424.4 %reduce-scatter.5.cloned.1.call-start = ((), (), s32[]{:S(2)}) async-start(), calls=%async_computation.7 | async-start | bytes 2621440 | tf_op jit(solution)/shard_map/reduce_scatter | solution.py:120
  226.0 87.9 %collective-permute-start = (bf16[128,3584]{1,0:T(8,128)(2,1)}, bf16[128,3584]{1,0:T(8,128)(2,1)S(1)}, u32[]{:S(2)}, u32[]{:S(2)}) collective-permute-start(bf16[128,3584]{1,0:T(8,128)(2,1)} %get-tuple-element.20), channel_id=1, source_target_pairs={{0,4},{4,8},{8,12},{12,16},{16,20},{20,24},{24,28},{28,0},{1,5},{5... | collective-permute-start | bytes 2752520 | tf_op jit(solution)/shard_map/ppermute | solution.py:87
  302.0 5.4 copy-start.6
  314.0 61.6 %collective-permute-start.1 = (bf16[128,3584]{1,0:T(8,128)(2,1)S(1)}, bf16[128,3584]{1,0:T(8,128)(2,1)S(1)}, u32[]{:S(2)}, u32[]{:S(2)}) collective-permute-start(bf16[128,3584]{1,0:T(8,128)(2,1)S(1)} %collective-permute-done), channel_id=1, source_target_pairs={{0,4},{4,8},{8,12},{12,16},{16,20},{20,24},{24,28},{28,0},{1,5},{5... | collective-permute-start | bytes 2752520 | tf_op jit(solution)/shard_map/ppermute | solution.py:87
  375.6 41.6 %collective-permute-start.2 = (bf16[128,3584]{1,0:T(8,128)(2,1)S(1)}, bf16[128,3584]{1,0:T(8,128)(2,1)S(1)}, u32[]{:S(2)}, u32[]{:S(2)}) collective-permute-start(bf16[128,3584]{1,0:T(8,128)(2,1)S(1)} %collective-permute-done.1), channel_id=1, source_target_pairs={{0,4},{4,8},{8,12},{12,16},{16,20},{20,24},{24,28},{28,0},{1,5},{5... | collective-permute-start | bytes 2752520 | tf_op jit(solution)/shard_map/ppermute | solution.py:87
  417.2 20.5 %collective-permute-start.3 = (bf16[128,3584]{1,0:T(8,128)(2,1)S(1)}, bf16[128,3584]{1,0:T(8,128)(2,1)S(1)}, u32[]{:S(2)}, u32[]{:S(2)}) collective-permute-start(bf16[128,3584]{1,0:T(8,128)(2,1)S(1)} %collective-permute-done.2), channel_id=1, source_target_pairs={{0,4},{4,8},{8,12},{12,16},{16,20},{20,24},{24,28},{28,0},{1,5},{5... | collective-permute-start | bytes 2752520 | tf_op jit(solution)/shard_map/ppermute | solution.py:87
  437.7 20.5 %collective-permute-start.4 = (bf16[128,3584]{1,0:T(8,128)(2,1)S(1)}, bf16[128,3584]{1,0:T(8,128)(2,1)S(1)}, u32[]{:S(2)}, u32[]{:S(2)}) collective-permute-start(bf16[128,3584]{1,0:T(8,128)(2,1)S(1)} %collective-permute-done.3), channel_id=1, source_target_pairs={{0,4},{4,8},{8,12},{12,16},{16,20},{20,24},{24,28},{28,0},{1,5},{5... | collective-permute-start | bytes 2752520 | tf_op jit(solution)/shard_map/ppermute | solution.py:87
  458.3 20.5 %collective-permute-start.5 = (bf16[128,3584]{1,0:T(8,128)(2,1)S(1)}, bf16[128,3584]{1,0:T(8,128)(2,1)S(1)}, u32[]{:S(2)}, u32[]{:S(2)}) collective-permute-start(bf16[128,3584]{1,0:T(8,128)(2,1)S(1)} %collective-permute-done.4), channel_id=1, source_target_pairs={{0,4},{4,8},{8,12},{12,16},{16,20},{20,24},{24,28},{28,0},{1,5},{5... | collective-permute-start | bytes 2752520 | tf_op jit(solution)/shard_map/ppermute | solution.py:87
  478.8 18.0 %collective-permute-start.6 = (bf16[128,3584]{1,0:T(8,128)(2,1)S(1)}, bf16[128,3584]{1,0:T(8,128)(2,1)S(1)}, u32[]{:S(2)}, u32[]{:S(2)}) collective-permute-start(bf16[128,3584]{1,0:T(8,128)(2,1)S(1)} %collective-permute-done.5), channel_id=1, source_target_pairs={{0,4},{4,8},{8,12},{12,16},{16,20},{20,24},{24,28},{28,0},{1,5},{5... | collective-permute-start | bytes 2752520 | tf_op jit(solution)/shard_map/ppermute | solution.py:87
  504.9 14.2 %copy-start = (f32[8,128,1024]{2,1,0:T(8,128)S(1)}, f32[8,128,1024]{2,1,0:T(8,128)}, u32[]{:S(2)}) copy-start(f32[8,128,1024]{2,1,0:T(8,128)} %copy.27) | copy-start | bytes 12582916
  504.9 14.2 %copy-start.2 = (bf16[8,128,3584]{2,1,0:T(8,128)(2,1)S(1)}, bf16[8,128,3584]{2,1,0:T(8,128)(2,1)}, u32[]{:S(2)}) copy-start(bf16[8,128,3584]{2,1,0:T(8,128)(2,1)} %gather_fusion) | copy-start | bytes 22020100
  634.1 16.3 %copy-start.4 = (bf16[1024,1024]{1,0:T(8,128)(2,1)S(1)}, bf16[1024,1024]{1,0:T(8,128)(2,1)}, u32[]{:S(2)}) copy-start(bf16[1024,1024]{1,0:T(8,128)(2,1)} %fusion.2) | copy-start | bytes 6291460
  646.9 18.0 %all-to-all-start.1 = ((bf16[8,32,1024]{2,1,0:T(8,128)(2,1)}), bf16[8,32,1024]{2,1,0:T(8,128)(2,1)S(1)}, u32[]{:S(2)}, u32[]{:S(2)}) async-start(bf16[8,32,1024]{2,1,0:T(8,128)(2,1)} %reduce-scatter.5.cloned.1.call-done), calls=%async_computation.3 | async-start | bytes 1048576 | tf_op jit(solution)/shard_map/all_to_all | solution.py:123
Sparse Core Ops, SparseCore 0:
  76.6 131.8 reduce-scatter.2
  214.2 183.3 all-gather.2
  399.8 209.1 all-gather.4
  611.4 29.5 reduce-scatter.4
